TPU v7x, 32 devices: a whole 2x2x4 slice. The times are simulated.
32 devices in a mesh: dp: 8 (over y, x, core), own: 4 (over z).
Axes of the slice: x: 2, y: 2, z: 4, core: 2. Of those that a mesh axis runs over, the one named last changes fastest.
Arguments:
- grads: bfloat16 [8, 6, 8192, 128], P('dp', None, 'own'), may hold values from -6 to 6
- proj: bfloat16 [4, 3, 8192, 1024], P('own', None, 'dp'), may hold values from -0.0625 to 0.0625
- moment1: float32 [4, 3, 1024, 128], P('own', None, 'dp'), may hold values from -24 to 24
- moment2: float32 [4, 3, 1024, 128], P('own', None, 'dp'), may hold values from 0.05 to 5
- plan: int32 [6], replicated, may hold values from 0 to 3, as said below
Outputs:
- update: bfloat16 [6, 8192, 128], P(None, 'own')
- new_moment1: float32 [4, 3, 1024, 128], P('own', None, 'dp')
- new_moment2: float32 [4, 3, 1024, 128], P('own', None, 'dp')
Inputs may be any that keep to these rules, and one draw needn't show every extreme that they name: `plan`: no owner is named more than 3 times, and some owner is named exactly 3 times.
All inputs are finite; a program needn't handle non-finite values.
Results may differ from a plain program's by a relative error of at most 0.015.
Values may be sent and summed in bfloat16 or wider, within the bound.
A program may use at most 64 MiB of HBM per device.

v0:
```python
import jax
import jax.numpy as jnp
from jax import lax
from jax.sharding import PartitionSpec as P

beta_one = 0.9
beta_two = 0.999
adam_eps = 1e-08
norm_eps = 1e-06
correct_one = 1.0 - 0.9**10
correct_two = 1.0 - 0.999**10


def slot_selector(plan, owner_count, capacity):
    matrices = plan.shape[0]
    places = jnp.arange(owner_count * capacity, dtype=jnp.int32)
    owners = places // capacity
    within = places % capacity
    index = jnp.arange(matrices, dtype=jnp.int32)
    before = jnp.sum(
        ((plan[None, :] == plan[:, None]) & (index[None, :] < index[:, None])).astype(jnp.int32),
        axis=1,
    )
    chosen = (plan[None, :] == owners[:, None]) & (before[None, :] == within[:, None])
    return chosen.astype(jnp.bfloat16)


def adam_moments(rank_share, first_old, second_old):
    first_new = beta_one * first_old + (1.0 - beta_one) * rank_share
    second_new = beta_two * second_old + (1.0 - beta_two) * rank_share * rank_share
    adam_step = first_new / correct_one / (jnp.sqrt(second_new / correct_two) + adam_eps)
    return (first_new, second_new, adam_step.astype(jnp.bfloat16))


def local(grads, proj, moment1, moment2, plan):
    owner_count = lax.axis_size("own")
    replica_count = lax.axis_size("dp")
    capacity = proj.shape[1]
    own_rows = grads.shape[2]
    columns = grads.shape[3]
    rank_rows = moment1.shape[2]
    selector = slot_selector(plan, owner_count, capacity)
    outgoing = jnp.einsum(
        "sj,jdc->sdc", selector, grads[0], preferred_element_type=jnp.float32
    ).astype(jnp.bfloat16)
    group_ratio = replica_count // owner_count
    piece_rows = own_rows // replica_count
    blocked = outgoing.reshape(owner_count * capacity, replica_count, piece_rows, columns)
    pieces = lax.psum_scatter(blocked, "dp", scatter_dimension=1, tiled=True).astype(jnp.float32)
    pieces = pieces.reshape(owner_count, capacity, piece_rows, columns)
    routed = lax.all_to_all(
        pieces.astype(jnp.bfloat16), "own", split_axis=0, concat_axis=0, tiled=True
    ).astype(pieces.dtype)
    span_pos = lax.axis_index("dp") // owner_count
    marker = (jnp.arange(group_ratio, dtype=jnp.int32) == span_pos).astype(jnp.float32)
    placed = routed[:, None] * marker[None, :, None, None, None]
    placed = placed.reshape(replica_count, capacity, piece_rows, columns)
    received = lax.all_to_all(
        placed.astype(jnp.bfloat16), "dp", split_axis=0, concat_axis=0, tiled=True
    ).astype(placed.dtype)
    received = received.reshape(group_ratio, owner_count, capacity, piece_rows, columns)
    mine = lax.axis_index("dp") % group_ratio
    kept = lax.dynamic_index_in_dim(received, mine, 0, keepdims=False)
    summed = jnp.transpose(kept, (1, 0, 2, 3)).reshape(capacity, owner_count * piece_rows, columns)
    grad_half = summed.astype(jnp.bfloat16)
    projection = proj[0]
    partial_value = jnp.einsum(
        "kdr,kdc->krc", projection, grad_half, preferred_element_type=jnp.float32
    )
    first_old = moment1[0]
    second_old = moment2[0]
    rank_full = lax.psum(partial_value.astype(jnp.bfloat16), "dp").astype(jnp.float32)
    rank_start = lax.axis_index("dp") * rank_rows
    rank_share = lax.dynamic_slice_in_dim(rank_full, rank_start, rank_rows, 1)
    first_new, second_new, adam_half = adam_moments(rank_share, first_old, second_old)
    adam_full = lax.all_gather(adam_half, "dp", axis=1, tiled=True)
    rank_half = rank_full.astype(jnp.bfloat16)
    grad_norms = jnp.sum(rank_full * rank_full, axis=1)
    adam_wide = adam_full.astype(jnp.float32)
    step_norms = jnp.sum(adam_wide * adam_wide, axis=1)
    column_scale = jnp.sqrt(step_norms) / (jnp.sqrt(grad_norms) + norm_eps)
    combined = (adam_wide - column_scale[:, None, :] * rank_half.astype(jnp.float32)).astype(
        jnp.bfloat16
    )
    update_full = (
        jnp.einsum("kdr,krc->kdc", projection, combined, preferred_element_type=jnp.float32)
        + column_scale[:, None, :] * summed
    )
    update_half = update_full.astype(jnp.bfloat16)
    gathered = lax.all_gather(update_half, "dp", axis=1, tiled=True)
    gathered = gathered.reshape(capacity, owner_count, own_rows, columns)
    returned = lax.all_to_all(gathered, "own", split_axis=1, concat_axis=0, tiled=True)
    slot_rows = returned.reshape(owner_count * capacity, own_rows, columns)
    update = jnp.einsum(
        "sj,sdc->jdc", selector, slot_rows, preferred_element_type=jnp.float32
    ).astype(jnp.bfloat16)
    return (update, first_new[None], second_new[None])


def solution(mesh):
    return jax.shard_map(
        local,
        mesh=mesh,
        in_specs=(
            P("dp", None, "own", None),
            P("own", None, "dp", None),
            P("own", None, "dp", None),
            P("own", None, "dp", None),
            P(),
        ),
        out_specs=(P(None, "own", None), P("own", None, "dp", None), P("own", None, "dp", None)),
        check_vma=False,
    )
```

profile of v0, /device:TPU:0, one launch (start us, length us, event | category | flops | bytes accessed | tf_op | source)
XLA Modules:
  0.0 447.2 jit_solution(17571062850924733432)
XLA Ops:
  7.2 0.0 copy-start
  7.2 0.0 reduce-scatter.2.cloned.1.call-start
  7.2 1.0 convert_reduce_fusion
  8.2 0.8 copy-done
  9.1 13.2 %convolution_convert_fusion = bf16[12,2048,128]{2,0,1:T(8,128)(2,1)S(1)} fusion(bf16[6,2048,128]{2,1,0:T(8,128)(2,1)S(1)} %bitcast.60, s32[12]{0:T(128)S(1)} %get-tuple-element.18, s32[12]{0:T(128)S(1)} %get-tuple-element.19, s32[6]{0:T(128)S(1)} %convert_reduce_fusion, s32[6]{0:T(128)} %param.9), kind=kOutput, calls=%fused_computation.2 | convolution fusion | flops 40894680 | bytes 9437328 | tf_op jit(solution)/shard_map/sj,jdc->sdc/dot_general | solution.py:43
  22.3 4.4 copy.37
  26.8 0.0 reduce-scatter.2.cloned.1.call-update
  26.8 64.6 %reduce-scatter.2.cloned.1.call-done = bf16[12,1,256,128]{3,2,0,1:T(8,128)(2,1)} async-done(((bf16[12,8,256,128]{3,2,0,1:T(8,128)(2,1)}), bf16[12,1,256,128]{3,2,0,1:T(8,128)(2,1)}) %reduce-scatter.2.cloned.1.call-update) | async-done | bytes 786448 | tf_op jit(solution)/shard_map/reduce_scatter | solution.py:49
  91.4 4.6 %all-to-all-start = ((bf16[4,3,256,128]{3,2,1,0:T(8,128)(2,1)}), bf16[4,3,256,128]{3,2,1,0:T(8,128)(2,1)S(1)}, u32[]{:S(2)}, u32[]{:S(2)}) async-start(bf16[4,3,256,128]{3,2,1,0:T(8,128)(2,1)} %bitcast.63), calls=%async_computation.1 | async-start | bytes 1572864 | tf_op jit(solution)/shard_map/all_to_all | solution.py:51
  96.0 0.1 mul.82
  96.1 19.8 %all-to-all-done = bf16[4,3,256,128]{3,2,1,0:T(8,128)(2,1)S(1)} async-done(((bf16[4,3,256,128]{3,2,1,0:T(8,128)(2,1)}), bf16[4,3,256,128]{3,2,1,0:T(8,128)(2,1)S(1)}, u32[]{:S(2)}, u32[]{:S(2)}) %all-to-all-start) | async-done | bytes 786464 | tf_op jit(solution)/shard_map/all_to_all | solution.py:51
  116.0 0.1 convert_element_type.58
  116.1 1.6 fusion.7
  117.7 3.6 all-to-all-start.1
  121.3 0.0 all-reduce.2.cloned.1.call-start
  121.3 20.9 %all-to-all-done.1 = bf16[8,3,256,128]{3,2,1,0:T(8,128)(2,1)S(1)} async-done(((bf16[8,3,256,128]{3,2,1,0:T(8,128)(2,1)}), bf16[8,3,256,128]{3,2,1,0:T(8,128)(2,1)S(1)}, u32[]{:S(2)}, u32[]{:S(2)}) %all-to-all-start.1) | async-done | bytes 1572896 | tf_op jit(solution)/shard_map/all_to_all | solution.py:58
  142.2 0.1 convert_bitcast_fusion
  142.4 0.8 copy.38
  143.2 0.8 reshape.73
  144.0 0.0 copy-start.3
  144.0 0.0 copy-start.4
  144.0 4.7 %fusion.19 = bf16[3,1024,128]{1,2,0:T(8,128)(2,1)} fusion(bf16[1,3,1024,1024]{3,2,1,0:T(8,128)(2,1)} %param.6, f32[3,1024,128]{1,2,0:T(8,128)S(1)} %reshape.73), kind=kOutput, calls=%fused_computation.20 | convolution fusion | flops 806092800 | bytes 8650752 | tf_op jit(solution)/shard_map/kdr,kdc->krc/dot_general | solution.py:67
  148.8 0.0 all-reduce.2.cloned.1.call-update
  148.8 0.0 all-gather.2.cloned.1.call-start
  148.8 0.0 copy-done.3
  148.8 0.1 copy.35
  149.0 0.0 copy-done.4
  149.0 0.1 copy.39
  149.1 52.7 %all-reduce.2.cloned.1.call-done = bf16[3,1024,128]{1,2,0:T(8,128)(2,1)} async-done(((bf16[3,1024,128]{1,2,0:T(8,128)(2,1)}), bf16[3,1024,128]{1,2,0:T(8,128)(2,1)}) %all-reduce.2.cloned.1.call-update) | async-done | bytes 786448 | tf_op jit(solution)/shard_map/psum | solution.py:72
  201.8 0.0 copy-start.2
  201.8 1.4 convert_element_type.64
  203.2 0.2 fusion.28
  203.4 10.0 %all_gather.6 = bf16[3,1024,128]{1,2,0:T(8,128)(2,1)S(1)} all-gather(bf16[3,128,128]{1,2,0:T(8,128)(2,1)S(1)} %get-tuple-element.16), channel_id=1, replica_groups=mesh['dp'=8,'own'=4] {'dp'}, dimensions={1}, use_global_device_ids=true | all-gather | bytes 884736 | tf_op jit(solution)/shard_map/all_gather | solution.py:76
  213.4 0.2 fusion.11
  213.6 0.0 copy-done.2
  213.6 0.2 multiply_reduce_fusion
  213.9 5.9 %fusion.13 = bf16[3,1024,128]{1,2,0:T(8,128)(2,1)} fusion(f32[3,1024,128]{1,2,0:T(8,128)S(1)} %reshape.73, bf16[1,3,1024,1024]{3,2,1,0:T(8,128)(2,1)} %param.6, bf16[3,1024,128]{1,2,0:T(8,128)(2,1)S(1)} %all_gather.6, f32[3,128]{1,0:T(4,128)S(1)} %add_divide_fusion, bf16[3,1024,128]{1,2,0:T(8,128)(2,1)S(1)} %copy-done.2), kind=kOutput, calls=%fused_computation.17 | convolution fusion | flops 808452096 | bytes 10225152 | tf_op jit(solution)/shard_map/kdr,krc->kdc/dot_general | solution.py:86
  219.8 0.0 all-gather.2.cloned.1.call-update
  219.8 45.6 %all-gather.2.cloned.1.call-done = bf16[3,8192,128]{1,2,0:T(8,128)(2,1)} async-done(((bf16[3,1024,128]{1,2,0:T(8,128)(2,1)}), bf16[3,8192,128]{1,2,0:T(8,128)(2,1)}) %all-gather.2.cloned.1.call-update) | async-done | bytes 6291472 | tf_op jit(solution)/shard_map/all_gather | solution.py:90
  265.4 11.1 %reshape.74 = bf16[3,4,2048,128]{2,1,3,0:T(4,128)(2,1)} reshape(bf16[3,8192,128]{1,2,0:T(8,128)(2,1)} %all-gather.2.cloned.1.call-done) | data formatting | bytes 12582912 | tf_op jit(solution)/shard_map/reshape | solution.py:91
  276.5 11.2 %copy.40 = bf16[3,4,2048,128]{3,2,0,1:T(8,128)(2,1)} copy(bf16[3,4,2048,128]{2,1,3,0:T(4,128)(2,1)} %reshape.74) | data formatting | bytes 12582912 | tf_op jit(solution)/shard_map/reshape | solution.py:91
  287.7 0.0 copy-start.5
  287.7 5.4 %all-to-all-start.2 = ((bf16[3,4,2048,128]{3,2,0,1:T(8,128)(2,1)}), bf16[3,4,2048,128]{3,2,0,1:T(8,128)(2,1)}, u32[]{:S(2)}, u32[]{:S(2)}) async-start(bf16[3,4,2048,128]{3,2,0,1:T(8,128)(2,1)} %copy.40), calls=%async_computation.3 | async-start | bytes 12582912 | tf_op jit(solution)/shard_map/all_to_all | solution.py:92
  293.1 0.8 copy.43
  293.9 0.8 copy.44
  294.7 137.2 %all-to-all-done.2 = bf16[3,4,2048,128]{3,2,0,1:T(8,128)(2,1)} async-done(((bf16[3,4,2048,128]{3,2,0,1:T(8,128)(2,1)}), bf16[3,4,2048,128]{3,2,0,1:T(8,128)(2,1)}, u32[]{:S(2)}, u32[]{:S(2)}) %all-to-all-start.2) | async-done | bytes 6291488 | tf_op jit(solution)/shard_map/all_to_all | solution.py:92
  431.9 0.0 copy-done.5
  431.9 0.0 copy-start.1
  431.9 6.7 %fusion.8 = bf16[6,2048,128]{2,0,1:T(8,128)(2,1)S(1)} fusion(bf16[12,2048,128]{2,1,0:T(8,128)(2,1)} %bitcast.15, s32[12]{0:T(128)S(1)} %get-tuple-element.18, s32[12]{0:T(128)S(1)} %get-tuple-element.19, s32[6]{0:T(128)S(1)} %convert_reduce_fusion, s32[6]{0:T(128)S(1)} %copy-done.5), kind=kOutput, calls=%fused_computation.10 | convolution fusion | flops 39321816 | bytes 9437328 | tf_op jit(solution)/shard_map/sj,sdc->jdc/dot_general | solution.py:94
  438.6 2.1 copy.42
  440.7 0.0 copy-done.1
  (4 shorter events, 0.0 us)
Async XLA Ops:
  7.2 1.9 copy-start
  7.2 84.2 %reduce-scatter.2.cloned.1.call-start = ((), (), s32[]{:S(2)}) async-start(), calls=%async_computation.4 | async-start | bytes 7077888 | tf_op jit(solution)/shard_map/reduce_scatter | solution.py:49
  91.4 24.6 %all-to-all-start = ((bf16[4,3,256,128]{3,2,1,0:T(8,128)(2,1)}), bf16[4,3,256,128]{3,2,1,0:T(8,128)(2,1)S(1)}, u32[]{:S(2)}, u32[]{:S(2)}) async-start(bf16[4,3,256,128]{3,2,1,0:T(8,128)(2,1)} %bitcast.63), calls=%async_computation.1 | async-start | bytes 1572864 | tf_op jit(solution)/shard_map/all_to_all | solution.py:51
  117.7 24.5 %all-to-all-start.1 = ((bf16[8,3,256,128]{3,2,1,0:T(8,128)(2,1)}), bf16[8,3,256,128]{3,2,1,0:T(8,128)(2,1)S(1)}, u32[]{:S(2)}, u32[]{:S(2)}) async-start(bf16[8,3,256,128]{3,2,1,0:T(8,128)(2,1)} %fusion.7), calls=%async_computation.2 | async-start | bytes 3145728 | tf_op jit(solution)/shard_map/all_to_all | solution.py:58
  121.3 80.5 %all-reduce.2.cloned.1.call-start = ((), (), s32[]{:S(2)}) async-start(), calls=%async_computation.5 | async-start | bytes 1572864 | tf_op jit(solution)/shard_map/psum | solution.py:72
  144.0 4.8 %copy-start.3 = (f32[1,3,128,128]{3,2,1,0:T(8,128)S(1)}, f32[1,3,128,128]{3,2,1,0:T(8,128)}, u32[]{:S(2)}) copy-start(f32[1,3,128,128]{3,2,1,0:T(8,128)} %param.7) | copy-start | bytes 589828
  144.0 4.9 %copy-start.4 = (f32[1,3,128,128]{3,2,1,0:T(8,128)S(1)}, f32[1,3,128,128]{3,2,1,0:T(8,128)}, u32[]{:S(2)}) copy-start(f32[1,3,128,128]{3,2,1,0:T(8,128)} %param.8) | copy-start | bytes 589828
  148.8 116.6 %all-gather.2.cloned.1.call-start = ((), (), s32[]{:S(2)}) async-start(), calls=%async_computation.6 | async-start | bytes 7077888 | tf_op jit(solution)/shard_map/all_gather | solution.py:90
  201.8 11.8 %copy-start.2 = (bf16[3,1024,128]{1,2,0:T(8,128)(2,1)S(1)}, bf16[3,1024,128]{1,2,0:T(8,128)(2,1)}, u32[]{:S(2)}) copy-start(bf16[3,1024,128]{1,2,0:T(8,128)(2,1)} %all-reduce.2.cloned.1.call-done) | copy-start | bytes 2359300
  287.7 144.2 %copy-start.5 = (s32[6]{0:T(128)S(1)}, s32[6]{0:T(128)}, u32[]{:S(2)}) copy-start(s32[6]{0:T(128)} %param.9) | copy-start | bytes 76
  287.7 144.2 %all-to-all-start.2 = ((bf16[3,4,2048,128]{3,2,0,1:T(8,128)(2,1)}), bf16[3,4,2048,128]{3,2,0,1:T(8,128)(2,1)}, u32[]{:S(2)}, u32[]{:S(2)}) async-start(bf16[3,4,2048,128]{3,2,0,1:T(8,128)(2,1)} %copy.40), calls=%async_computation.3 | async-start | bytes 12582912 | tf_op jit(solution)/shard_map/all_to_all | solution.py:92
  431.9 8.7 %copy-start.1 = (bf16[1,6,2048,128]{3,2,1,0:T(8,128)(2,1)S(1)}, bf16[1,6,2048,128]{3,2,1,0:T(8,128)(2,1)}, u32[]{:S(2)}) copy-start(bf16[1,6,2048,128]{3,2,1,0:T(8,128)(2,1)} %param.5) | copy-start | bytes 9437188
Sparse Core Ops, SparseCore 0:
  26.9 64.4 reduce-scatter.1
  148.9 52.8 all-reduce.1
  219.9 45.3 all-gather.1
where the time goes:
time: 448 us; the launch traced here: 447 us
  waiting for transfers between devices  341 us (76%)
  local copies, waits for them, and re-layouts  33.4 us (7%)
  matrix products  30.5 us (7%)
  between operations  13.9 us (3%)
  starting transfers between devices  13.7 us (3%)
  blocking collectives  10 us (2%)
  other arithmetic  4.87 us (1%)
    all_to_all x1, waiting for transfers between devices, local(): lax.all_to_all(gathered, 'own', split_axis=1, concat_axis=0, tiled=True)  137 us
    reduce_scatter x1, waiting for transfers between devices, local(): lax.psum_scatter(blocked, 'dp', scatter_dimension=1, tiled=True)  64.6 us
    psum x1, waiting for transfers between devices, local(): lax.psum(partial_value.astype(jnp.bfloat16), 'dp').astype(jnp.float32)  52.7 us
    all_gather x1, waiting for transfers between devices, local(): gathered = lax.all_gather(update_half, 'dp', axis=1, tiled=True)  45.6 us
    reshape x2, local copies, waits for them, and re-layouts, local(): gathered = gathered.reshape(capacity, owner_count, own_rows, columns)  22.4 us
    all_to_all x1, waiting for transfers between devices, local(): lax.all_to_all(placed.astype(jnp.bfloat16), 'dp', split_axis=0, concat_ax...  20.9 us
    all_to_all x1, waiting for transfers between devices, local(): lax.all_to_all(pieces.astype(jnp.bfloat16), 'own', split_axis=0, concat_a...  19.8 us
    dot_general x1, matrix products, local(): jnp.einsum('sj,jdc->sdc', selector, grads[0], preferred_element_type=jnp....  13.2 us
  transfers between devices with their start and end apart: 6, of which 6 were waited for; matrix products, arithmetic and copies ran while one was open for 0% of the time, Pallas kernels for 0%

commit v1 on v0

--- a/solution.py
+++ b/solution.py
@@ -87,7 +87,7 @@
         + column_scale[:, None, :] * summed
     )
     update_half = update_full.astype(jnp.bfloat16)
-    gathered = lax.all_gather(update_half, "dp", axis=1, tiled=True)
+    gathered = jnp.concatenate(lax.all_gather(update_half, "dp"), axis=1)
     gathered = gathered.reshape(capacity, owner_count, own_rows, columns)
     returned = lax.all_to_all(gathered, "own", split_axis=1, concat_axis=0, tiled=True)
     slot_rows = returned.reshape(owner_count * capacity, own_rows, columns)

time: 448 us -> 434 us (0.969)
  local copies, waits for them, and re-layouts: 33.4 us -> 19.6 us
    reshape x2 -> x1, local copies, waits for them, and re-layouts: 22.4 us -> 3.2 us  [local(): gathered = jnp.concatenate(lax.all_gather(update_half, 'dp'), axis=1)]
where the time goes in v1:
time: 434 us; the launch traced here: 433 us
  waiting for transfers between devices  341 us (79%)
  matrix products  30.5 us (7%)
  local copies, waits for them, and re-layouts  19.6 us (5%)
  between operations  13.9 us (3%)
  starting transfers between devices  13.7 us (3%)
  blocking collectives  10 us (2%)
  other arithmetic  4.87 us (1%)
    all_to_all x1, waiting for transfers between devices, local(): lax.all_to_all(gathered, 'own', split_axis=1, concat_axis=0, tiled=True)  137 us
    reduce_scatter x1, waiting for transfers between devices, local(): lax.psum_scatter(blocked, 'dp', scatter_dimension=1, tiled=True)  64.6 us
    psum x1, waiting for transfers between devices, local(): lax.psum(partial_value.astype(jnp.bfloat16), 'dp').astype(jnp.float32)  52.7 us
    all_gather x1, waiting for transfers between devices, local(): gathered = jnp.concatenate(lax.all_gather(update_half, 'dp'), axis=1)  45.6 us
    all_to_all x1, waiting for transfers between devices, local(): lax.all_to_all(placed.astype(jnp.bfloat16), 'dp', split_axis=0, concat_ax...  20.9 us
    all_to_all x1, waiting for transfers between devices, local(): lax.all_to_all(pieces.astype(jnp.bfloat16), 'own', split_axis=0, concat_a...  19.8 us
    dot_general x1, matrix products, local(): jnp.einsum('sj,jdc->sdc', selector, grads[0], preferred_element_type=jnp....  13.2 us
    all_gather x1, blocking collectives, local(): adam_full = lax.all_gather(adam_half, 'dp', axis=1, tiled=True)  10 us
  transfers between devices with their start and end apart: 6, of which 6 were waited for; matrix products, arithmetic and copies ran while one was open for 0% of the time, Pallas kernels for 0%

profile of v1, /device:TPU:0, one launch (start us, length us, event | category | flops | bytes accessed | tf_op | source)
XLA Modules:
  0.0 433.4 jit_solution(5833051217029918127)
XLA Ops:
  7.2 0.0 copy-start
  7.2 0.0 reduce-scatter.2.cloned.1.call-start
  7.2 1.0 convert_reduce_fusion
  8.2 0.8 copy-done
  9.1 13.2 %convolution_convert_fusion = bf16[12,2048,128]{2,0,1:T(8,128)(2,1)S(1)} fusion(bf16[6,2048,128]{2,1,0:T(8,128)(2,1)S(1)} %bitcast.62, s32[12]{0:T(128)S(1)} %get-tuple-element.24, s32[12]{0:T(128)S(1)} %get-tuple-element.25, s32[6]{0:T(128)S(1)} %convert_reduce_fusion, s32[6]{0:T(128)} %param.9), kind=kOutput, calls=%fused_computation.2 | convolution fusion | flops 40894680 | bytes 9437328 | tf_op jit(solution)/shard_map/sj,jdc->sdc/dot_general | solution.py:43
  22.3 4.4 %copy.61 = bf16[12,8,256,128]{3,2,0,1:T(8,128)(2,1)} copy(bf16[12,8,256,128]{3,0,2,1:T(8,128)(2,1)S(1)} %bitcast.63) | data formatting | bytes 12582912 | tf_op jit(solution)/shard_map/reshape | solution.py:48
  26.8 0.0 reduce-scatter.2.cloned.1.call-update
  26.8 64.6 %reduce-scatter.2.cloned.1.call-done = bf16[12,1,256,128]{3,2,0,1:T(8,128)(2,1)} async-done(((bf16[12,8,256,128]{3,2,0,1:T(8,128)(2,1)}), bf16[12,1,256,128]{3,2,0,1:T(8,128)(2,1)}) %reduce-scatter.2.cloned.1.call-update) | async-done | bytes 786448 | tf_op jit(solution)/shard_map/reduce_scatter | solution.py:49
  91.4 4.6 %all-to-all-start = ((bf16[4,3,256,128]{3,2,1,0:T(8,128)(2,1)}), bf16[4,3,256,128]{3,2,1,0:T(8,128)(2,1)S(1)}, u32[]{:S(2)}, u32[]{:S(2)}) async-start(bf16[4,3,256,128]{3,2,1,0:T(8,128)(2,1)} %bitcast.67), calls=%async_computation.1 | async-start | bytes 1572864 | tf_op jit(solution)/shard_map/all_to_all | solution.py:51
  96.0 0.1 mul.82
  96.1 19.8 %all-to-all-done = bf16[4,3,256,128]{3,2,1,0:T(8,128)(2,1)S(1)} async-done(((bf16[4,3,256,128]{3,2,1,0:T(8,128)(2,1)}), bf16[4,3,256,128]{3,2,1,0:T(8,128)(2,1)S(1)}, u32[]{:S(2)}, u32[]{:S(2)}) %all-to-all-start) | async-done | bytes 786464 | tf_op jit(solution)/shard_map/all_to_all | solution.py:51
  116.0 0.1 convert_element_type.58
  116.1 1.6 fusion.7
  117.7 3.6 all-to-all-start.1
  121.3 0.0 all-reduce.2.cloned.1.call-start
  121.3 20.9 %all-to-all-done.1 = bf16[8,3,256,128]{3,2,1,0:T(8,128)(2,1)S(1)} async-done(((bf16[8,3,256,128]{3,2,1,0:T(8,128)(2,1)}), bf16[8,3,256,128]{3,2,1,0:T(8,128)(2,1)S(1)}, u32[]{:S(2)}, u32[]{:S(2)}) %all-to-all-start.1) | async-done | bytes 1572896 | tf_op jit(solution)/shard_map/all_to_all | solution.py:58
  142.2 0.1 convert_bitcast_fusion
  142.4 0.8 copy.62
  143.2 0.8 reshape.73
  144.0 0.0 copy-start.3
  144.0 0.0 copy-start.4
  144.0 4.7 %fusion.19 = bf16[3,1024,128]{1,2,0:T(8,128)(2,1)} fusion(bf16[1,3,1024,1024]{3,2,1,0:T(8,128)(2,1)} %param.6, f32[3,1024,128]{1,2,0:T(8,128)S(1)} %reshape.73), kind=kOutput, calls=%fused_computation.20 | convolution fusion | flops 806092800 | bytes 8650752 | tf_op jit(solution)/shard_map/kdr,kdc->krc/dot_general | solution.py:67
  148.8 0.0 all-reduce.2.cloned.1.call-update
  148.8 0.0 all-gather.3.cloned.1.call-start
  148.8 0.0 copy-done.3
  148.8 0.1 copy.59
  149.0 0.0 copy-done.4
  149.0 0.1 copy.63
  149.1 52.7 %all-reduce.2.cloned.1.call-done = bf16[3,1024,128]{1,2,0:T(8,128)(2,1)} async-done(((bf16[3,1024,128]{1,2,0:T(8,128)(2,1)}), bf16[3,1024,128]{1,2,0:T(8,128)(2,1)}) %all-reduce.2.cloned.1.call-update) | async-done | bytes 786448 | tf_op jit(solution)/shard_map/psum | solution.py:72
  201.8 0.0 copy-start.2
  201.8 1.4 convert_element_type.64
  203.2 0.2 fusion.28
  203.4 10.0 %all_gather.9 = bf16[3,1024,128]{1,2,0:T(8,128)(2,1)S(1)} all-gather(bf16[3,128,128]{1,2,0:T(8,128)(2,1)S(1)} %get-tuple-element.22), channel_id=1, replica_groups=mesh['dp'=8,'own'=4] {'dp'}, dimensions={1}, use_global_device_ids=true | all-gather | bytes 884736 | tf_op jit(solution)/shard_map/all_gather | solution.py:76
  213.4 0.2 fusion.11
  213.6 0.0 copy-done.2
  213.6 0.2 multiply_reduce_fusion
  213.9 5.9 %fusion.13 = bf16[3,1024,128]{1,2,0:T(8,128)(2,1)} fusion(f32[3,1024,128]{1,2,0:T(8,128)S(1)} %reshape.73, bf16[1,3,1024,1024]{3,2,1,0:T(8,128)(2,1)} %param.6, bf16[3,1024,128]{1,2,0:T(8,128)(2,1)S(1)} %all_gather.9, f32[3,128]{1,0:T(4,128)S(1)} %add_divide_fusion, bf16[3,1024,128]{1,2,0:T(8,128)(2,1)S(1)} %copy-done.2), kind=kOutput, calls=%fused_computation.17 | convolution fusion | flops 808452096 | bytes 10225152 | tf_op jit(solution)/shard_map/kdr,krc->kdc/dot_general | solution.py:86
  219.8 2.3 copy.64
  222.1 0.0 all-gather.3.cloned.1.call-update
  222.1 45.6 %all-gather.3.cloned.1.call-done = bf16[24,1024,128]{2,1,0:T(8,128)(2,1)} async-done(((bf16[3,1024,128]{2,1,0:T(8,128)(2,1)}), bf16[24,1024,128]{2,1,0:T(8,128)(2,1)}) %all-gather.3.cloned.1.call-update) | async-done | bytes 6291472 | tf_op jit(solution)/shard_map/all_gather | solution.py:90
  267.7 3.2 copy.65
  270.9 3.1 copy.66
  274.0 0.0 copy-start.5
  274.0 5.4 %all-to-all-start.2 = ((bf16[3,4,2048,128]{3,2,0,1:T(8,128)(2,1)}), bf16[3,4,2048,128]{3,2,0,1:T(8,128)(2,1)}, u32[]{:S(2)}, u32[]{:S(2)}) async-start(bf16[3,4,2048,128]{3,2,0,1:T(8,128)(2,1)} %copy.66), calls=%async_computation.3 | async-start | bytes 12582912 | tf_op jit(solution)/shard_map/all_to_all | solution.py:92
  279.3 0.8 copy.69
  280.1 0.8 copy.70
  280.9 137.2 %all-to-all-done.2 = bf16[3,4,2048,128]{3,2,0,1:T(8,128)(2,1)} async-done(((bf16[3,4,2048,128]{3,2,0,1:T(8,128)(2,1)}), bf16[3,4,2048,128]{3,2,0,1:T(8,128)(2,1)}, u32[]{:S(2)}, u32[]{:S(2)}) %all-to-all-start.2) | async-done | bytes 6291488 | tf_op jit(solution)/shard_map/all_to_all | solution.py:92
  418.2 0.0 copy-done.5
  418.2 0.0 copy-start.1
  418.2 6.7 %fusion.8 = bf16[6,2048,128]{2,0,1:T(8,128)(2,1)S(1)} fusion(bf16[12,2048,128]{2,1,0:T(8,128)(2,1)} %bitcast.18, s32[12]{0:T(128)S(1)} %get-tuple-element.24, s32[12]{0:T(128)S(1)} %get-tuple-element.25, s32[6]{0:T(128)S(1)} %convert_reduce_fusion, s32[6]{0:T(128)S(1)} %copy-done.5), kind=kOutput, calls=%fused_computation.10 | convolution fusion | flops 39321816 | bytes 9437328 | tf_op jit(solution)/shard_map/sj,sdc->jdc/dot_general | solution.py:94
  424.8 2.1 copy.68
  426.9 0.0 copy-done.1
  (4 shorter events, 0.0 us)
Async XLA Ops:
  7.2 1.9 copy-start
  7.2 84.2 %reduce-scatter.2.cloned.1.call-start = ((), (), s32[]{:S(2)}) async-start(), calls=%async_computation.4 | async-start | bytes 7077888 | tf_op jit(solution)/shard_map/reduce_scatter | solution.py:49
  91.4 24.6 %all-to-all-start = ((bf16[4,3,256,128]{3,2,1,0:T(8,128)(2,1)}), bf16[4,3,256,128]{3,2,1,0:T(8,128)(2,1)S(1)}, u32[]{:S(2)}, u32[]{:S(2)}) async-start(bf16[4,3,256,128]{3,2,1,0:T(8,128)(2,1)} %bitcast.67), calls=%async_computation.1 | async-start | bytes 1572864 | tf_op jit(solution)/shard_map/all_to_all | solution.py:51
  117.7 24.5 %all-to-all-start.1 = ((bf16[8,3,256,128]{3,2,1,0:T(8,128)(2,1)}), bf16[8,3,256,128]{3,2,1,0:T(8,128)(2,1)S(1)}, u32[]{:S(2)}, u32[]{:S(2)}) async-start(bf16[8,3,256,128]{3,2,1,0:T(8,128)(2,1)} %fusion.7), calls=%async_computation.2 | async-start | bytes 3145728 | tf_op jit(solution)/shard_map/all_to_all | solution.py:58
  121.3 80.5 %all-reduce.2.cloned.1.call-start = ((), (), s32[]{:S(2)}) async-start(), calls=%async_computation.5 | async-start | bytes 1572864 | tf_op jit(solution)/shard_map/psum | solution.py:72
  144.0 4.8 %copy-start.3 = (f32[1,3,128,128]{3,2,1,0:T(8,128)S(1)}, f32[1,3,128,128]{3,2,1,0:T(8,128)}, u32[]{:S(2)}) copy-start(f32[1,3,128,128]{3,2,1,0:T(8,128)} %param.7) | copy-start | bytes 589828
  144.0 4.9 %copy-start.4 = (f32[1,3,128,128]{3,2,1,0:T(8,128)S(1)}, f32[1,3,128,128]{3,2,1,0:T(8,128)}, u32[]{:S(2)}) copy-start(f32[1,3,128,128]{3,2,1,0:T(8,128)} %param.8) | copy-start | bytes 589828
  148.8 118.9 %all-gather.3.cloned.1.call-start = ((), (), s32[]{:S(2)}) async-start(), calls=%async_computation.6 | async-start | bytes 7077888 | tf_op jit(solution)/shard_map/all_gather | solution.py:90
  201.8 11.8 %copy-start.2 = (bf16[3,1024,128]{1,2,0:T(8,128)(2,1)S(1)}, bf16[3,1024,128]{1,2,0:T(8,128)(2,1)}, u32[]{:S(2)}) copy-start(bf16[3,1024,128]{1,2,0:T(8,128)(2,1)} %all-reduce.2.cloned.1.call-done) | copy-start | bytes 2359300
  274.0 144.2 %copy-start.5 = (s32[6]{0:T(128)S(1)}, s32[6]{0:T(128)}, u32[]{:S(2)}) copy-start(s32[6]{0:T(128)} %param.9) | copy-start | bytes 76
  274.0 144.2 %all-to-all-start.2 = ((bf16[3,4,2048,128]{3,2,0,1:T(8,128)(2,1)}), bf16[3,4,2048,128]{3,2,0,1:T(8,128)(2,1)}, u32[]{:S(2)}, u32[]{:S(2)}) async-start(bf16[3,4,2048,128]{3,2,0,1:T(8,128)(2,1)} %copy.66), calls=%async_computation.3 | async-start | bytes 12582912 | tf_op jit(solution)/shard_map/all_to_all | solution.py:92
  418.2 8.8 %copy-start.1 = (bf16[1,6,2048,128]{3,2,1,0:T(8,128)(2,1)S(1)}, bf16[1,6,2048,128]{3,2,1,0:T(8,128)(2,1)}, u32[]{:S(2)}) copy-start(bf16[1,6,2048,128]{3,2,1,0:T(8,128)(2,1)} %param.5) | copy-start | bytes 9437188
Sparse Core Ops, SparseCore 0:
  26.9 64.4 reduce-scatter.1
  148.9 52.8 all-reduce.1
  222.2 45.3 all-gather.2
